TPU v7x, 32 devices: a whole 2x2x4 slice. The times are simulated.
32 devices in a mesh: brow: 4 (over z), bcol: 8 (over y, x, core).
Axes of the slice: x: 2, y: 2, z: 4, core: 2. Of those that a mesh axis runs over, the one named last changes fastest.
Arguments:
- anc_tiles: int32 [1, 12], replicated, may hold values from 0 to 31, as said below
- ancestor_inverse: float32 [16384, 16384], P('brow', 'bcol'), as said below
- factor_pieces: float32 [16384, 1536], P('bcol', 'brow'), may hold values from -6 to 6
Outputs:
- inverse_rows: float32 [1536, 16384], P('bcol', 'brow')
Inputs may be any that keep to these rules, and one draw needn't show every extreme that they name: `anc_tiles`: each row lists 12 different tiles; tile 32 - 1 is listed in every row, tile 0 in row 0. ancestor_inverse is symmetric.
All inputs are finite; a program needn't handle non-finite values.
Results may differ from a plain program's by a relative error of at most 0.00007.
Values sent between devices are 32-bit elements; how exact they have to be, the bound alone decides.
A program may use at most 128 MiB of HBM per device.

v0:
```python
import jax
import jax.numpy as jnp
from jax import lax
from jax.sharding import PartitionSpec as P

TS = 512
W = 1536
A = 32
K = 1
CHUNKS = 4


def split(x):
    high = lax.reduce_precision(x, exponent_bits=8, mantissa_bits=7)
    return (high.astype(jnp.bfloat16), (x - high).astype(jnp.bfloat16))


def product(x, y, **kwargs):
    return lax.dot_general(
        x, y, (((1,), (1,)), ((), ())), preferred_element_type=jnp.float32, **kwargs
    )


def local(anc_tiles, ancestor_inverse, factor_pieces):
    col_index = lax.axis_index("bcol")
    row_index = lax.axis_index("brow")
    n_col = lax.axis_size("bcol")
    n_row = lax.axis_size("brow")
    block_rows, block_cols = ancestor_inverse.shape
    tiles_col, tiles_row = (block_cols // TS, block_rows // TS)
    total_cols = factor_pieces.shape[1] * n_row
    tile_ids = jnp.arange(A, dtype=jnp.int32)
    listed = jnp.any(anc_tiles[:, :, None] == tile_ids[None, None, :], axis=1)
    col_super = (row_index * factor_pieces.shape[1] + jnp.arange(factor_pieces.shape[1])) // W
    listed_col = lax.dynamic_slice_in_dim(listed, col_index * tiles_col, tiles_col, 1)
    col_mask = jnp.repeat(listed_col[col_super], TS, axis=1)
    factor = jnp.where(col_mask, factor_pieces.T, 0.0)
    width = total_cols // n_col // CHUNKS
    factor = factor.reshape(-1, CHUNKS, width, block_cols)
    gathered = [
        lax.all_gather(factor[:, q], "brow", axis=0, tiled=True).reshape(-1, block_cols)
        for q in range(CHUNKS)
    ]
    sums = []
    for q in range(CHUNKS):
        part = product(gathered[q], ancestor_inverse, precision=lax.Precision.HIGH)
        sums.append(lax.psum_scatter(part, "bcol", scatter_dimension=0, tiled=True))
    summed = jnp.concatenate(sums, axis=0)
    out_rows = summed.shape[0]
    row_super = (col_index * out_rows + jnp.arange(out_rows)) // W
    listed_row = lax.dynamic_slice_in_dim(listed, row_index * tiles_row, tiles_row, 1)
    out_mask = jnp.repeat(listed_row[row_super], TS, axis=1)
    return jnp.where(out_mask, -summed, 0.0)


def solution(mesh):
    in_specs = (P(), P("brow", "bcol"), P("bcol", "brow"))
    out_specs = P("bcol", "brow")
    return jax.shard_map(local, mesh=mesh, in_specs=in_specs, out_specs=out_specs, check_vma=False)
```

profile of v0, /device:TPU:0, one launch (start us, length us, event | category | flops | bytes accessed | tf_op | source)
XLA Modules:
  0.0 543.0 jit_solution(9109065422733536276)
XLA Ops:
  6.5 0.0 all-gather.15.cloned.1.call-start
  6.5 0.7 fusion.1
  7.3 0.1 dynamic-slice.7
  7.4 0.5 broadcast_in_dim.19
  7.8 1.3 copy.8
  9.2 2.4 copy.6
  11.6 1.6 bitcast_select_fusion
  13.2 1.8 fusion.2
  15.0 0.0 all-gather.15.cloned.1.call-update
  15.0 0.0 all-gather.9.cloned.1.call-start
  15.0 0.7 all-gather.9.cloned.1.call-update
  15.7 0.0 all-gather.11.cloned.1.call-start
  15.8 0.7 all-gather.11.cloned.1.call-update
  16.5 0.0 all-gather.13.cloned.1.call-start
  16.5 0.5 all-gather.13.cloned.1.call-update
  17.1 0.0 reduce-scatter.11.cloned.1.call-start
  17.1 64.2 %all-gather.15.cloned.1.call-done = f32[8,1,48,2048]{3,2,1,0:T(8,128)} async-done(((f32[2,1,48,2048]{3,2,1,0:T(8,128)}), f32[8,1,48,2048]{3,2,1,0:T(8,128)}) %all-gather.15.cloned.1.call-update) | async-done | bytes 3145744 | tf_op jit(solution)/shard_map/all_gather | solution.py:41
  81.4 26.1 %fusion.6 = f32[384,4096]{1,0:T(8,128)} fusion(f32[384,2048]{1,0:T(8,128)} %bitcast.24, f32[4096,2048]{1,0:T(8,128)} %param.4), kind=kOutput, calls=%fused_computation.9 | convolution fusion | flops 19327352832 | bytes 42991616 | tf_op jit(solution)/shard_map/dot_general | solution.py:19
  107.5 0.0 reduce-scatter.11.cloned.1.call-update
  107.5 0.2 reduce-scatter.5.cloned.1.call-start
  107.7 37.4 %all-gather.9.cloned.1.call-done = f32[8,1,48,2048]{3,2,1,0:T(8,128)} async-done(((f32[2,1,48,2048]{3,2,1,0:T(8,128)}), f32[8,1,48,2048]{3,2,1,0:T(8,128)}) %all-gather.9.cloned.1.call-update) | async-done | bytes 3145744 | tf_op jit(solution)/shard_map/all_gather | solution.py:41
  145.1 26.1 %fusion.3 = f32[384,4096]{1,0:T(8,128)} fusion(f32[384,2048]{1,0:T(8,128)} %bitcast.23, f32[4096,2048]{1,0:T(8,128)} %param.4), kind=kOutput, calls=%fused_computation.6 | convolution fusion | flops 19327352832 | bytes 42991616 | tf_op jit(solution)/shard_map/dot_general | solution.py:19
  171.2 0.0 reduce-scatter.5.cloned.1.call-update
  171.3 0.0 reduce-scatter.7.cloned.1.call-start
  171.3 37.5 %all-gather.11.cloned.1.call-done = f32[8,1,48,2048]{3,2,1,0:T(8,128)} async-done(((f32[2,1,48,2048]{3,2,1,0:T(8,128)}), f32[8,1,48,2048]{3,2,1,0:T(8,128)}) %all-gather.11.cloned.1.call-update) | async-done | bytes 3145744 | tf_op jit(solution)/shard_map/all_gather | solution.py:41
  208.9 26.1 %fusion.4 = f32[384,4096]{1,0:T(8,128)} fusion(f32[384,2048]{1,0:T(8,128)} %bitcast.22, f32[4096,2048]{1,0:T(8,128)} %param.4), kind=kOutput, calls=%fused_computation.7 | convolution fusion | flops 19327352832 | bytes 42991616 | tf_op jit(solution)/shard_map/dot_general | solution.py:19
  235.0 0.0 reduce-scatter.7.cloned.1.call-update
  235.0 0.3 reduce-scatter.9.cloned.1.call-start
  235.3 37.2 %all-gather.13.cloned.1.call-done = f32[8,1,48,2048]{3,2,1,0:T(8,128)} async-done(((f32[2,1,48,2048]{3,2,1,0:T(8,128)}), f32[8,1,48,2048]{3,2,1,0:T(8,128)}) %all-gather.13.cloned.1.call-update) | async-done | bytes 3145744 | tf_op jit(solution)/shard_map/all_gather | solution.py:41
  272.5 26.1 %fusion.5 = f32[384,4096]{1,0:T(8,128)} fusion(f32[384,2048]{1,0:T(8,128)} %bitcast.21, f32[4096,2048]{1,0:T(8,128)} %param.4), kind=kOutput, calls=%fused_computation.8 | convolution fusion | flops 19327352832 | bytes 42991616 | tf_op jit(solution)/shard_map/dot_general | solution.py:19
  298.6 0.0 reduce-scatter.9.cloned.1.call-update
  298.6 0.1 dynamic-slice.6
  298.7 0.3 broadcast_in_dim.18
  299.0 0.5 copy.7
  299.5 36.6 %reduce-scatter.11.cloned.1.call-done = f32[48,4096]{1,0:T(8,128)} async-done(((f32[384,4096]{1,0:T(8,128)}), f32[48,4096]{1,0:T(8,128)}) %reduce-scatter.11.cloned.1.call-update) | async-done | bytes 786448 | tf_op jit(solution)/shard_map/reduce_scatter | solution.py:47
  336.1 65.4 %reduce-scatter.5.cloned.1.call-done = f32[48,4096]{1,0:T(8,128)} async-done(((f32[384,4096]{1,0:T(8,128)}), f32[48,4096]{1,0:T(8,128)}) %reduce-scatter.5.cloned.1.call-update) | async-done | bytes 786448 | tf_op jit(solution)/shard_map/reduce_scatter | solution.py:47
  401.5 65.2 %reduce-scatter.7.cloned.1.call-done = f32[48,4096]{1,0:T(8,128)} async-done(((f32[384,4096]{1,0:T(8,128)}), f32[48,4096]{1,0:T(8,128)}) %reduce-scatter.7.cloned.1.call-update) | async-done | bytes 786448 | tf_op jit(solution)/shard_map/reduce_scatter | solution.py:47
  466.7 65.5 %reduce-scatter.9.cloned.1.call-done = f32[48,4096]{1,0:T(8,128)} async-done(((f32[384,4096]{1,0:T(8,128)}), f32[48,4096]{1,0:T(8,128)}) %reduce-scatter.9.cloned.1.call-update) | async-done | bytes 786448 | tf_op jit(solution)/shard_map/reduce_scatter | solution.py:47
  532.2 4.0 fusion
Async XLA Ops:
  6.5 74.8 %all-gather.15.cloned.1.call-start = ((), (), s32[]{:S(2)}) async-start(), calls=%async_computation.11 | async-start | bytes 3932160 | tf_op jit(solution)/shard_map/all_gather | solution.py:41
  15.0 130.1 %all-gather.9.cloned.1.call-start = ((), (), s32[]{:S(2)}) async-start(), calls=%async_computation.8 | async-start | bytes 3932160 | tf_op jit(solution)/shard_map/all_gather | solution.py:41
  15.7 193.1 %all-gather.11.cloned.1.call-start = ((), (), s32[]{:S(2)}) async-start(), calls=%async_computation.9 | async-start | bytes 3932160 | tf_op jit(solution)/shard_map/all_gather | solution.py:41
  16.5 256.0 %all-gather.13.cloned.1.call-start = ((), (), s32[]{:S(2)}) async-start(), calls=%async_computation.10 | async-start | bytes 3932160 | tf_op jit(solution)/shard_map/all_gather | solution.py:41
  17.1 319.1 %reduce-scatter.11.cloned.1.call-start = ((), (), s32[]{:S(2)}) async-start(), calls=%async_computation.7 | async-start | bytes 7077888 | tf_op jit(solution)/shard_map/reduce_scatter | solution.py:47
  107.5 294.0 %reduce-scatter.5.cloned.1.call-start = ((), (), s32[]{:S(2)}) async-start(), calls=%async_computation.4 | async-start | bytes 7077888 | tf_op jit(solution)/shard_map/reduce_scatter | solution.py:47
  171.3 295.4 %reduce-scatter.7.cloned.1.call-start = ((), (), s32[]{:S(2)}) async-start(), calls=%async_computation.5 | async-start | bytes 7077888 | tf_op jit(solution)/shard_map/reduce_scatter | solution.py:47
  235.0 297.2 %reduce-scatter.9.cloned.1.call-start = ((), (), s32[]{:S(2)}) async-start(), calls=%async_computation.6 | async-start | bytes 7077888 | tf_op jit(solution)/shard_map/reduce_scatter | solution.py:47
Sparse Core Ops, SparseCore 0:
  15.1 66.1 all-gather.14
  82.9 62.1 all-gather.8
  146.7 62.1 all-gather.10
  210.3 62.1 all-gather.12
  275.7 60.3 reduce-scatter.10
  339.7 61.7 reduce-scatter.4
  404.9 61.7 reduce-scatter.6
  470.4 61.7 reduce-scatter.8
where the time goes:
time: 543 us
  waiting for transfers between devices  411 us (76%)
  matrix products  105 us (19%)
  between operations  13.5 us (2%)
  local copies, waits for them, and re-layouts  6.92 us (1%)
  other arithmetic  6.4 us (1%)
    reduce_scatter x4, waiting for transfers between devices, local(): sums.append(lax.psum_scatter(part, 'bcol', scatter_dimension=0, tiled=True))  233 us
    all_gather x4, waiting for transfers between devices, local(): lax.all_gather(factor[:, q], 'brow', axis=0, tiled=True)  176 us
    dot_general x4, matrix products, product(): lax.dot_general(x, y, (((1,), (1,)), ((), ())), preferred_element_type=jn...  105 us
  transfers between devices with their start and end apart: 8, of which 8 were waited for; matrix products, arithmetic and copies ran while one was open for 19% of the time, Pallas kernels for 0%

commit v1 on v0

--- a/solution.py
+++ b/solution.py
@@ -8,6 +8,19 @@
 A = 32
 K = 1
 CHUNKS = 4
+
+
+def gather_around(x, axis, dim):
+    ways = lax.axis_size(axis)
+    up = [(d, (d + 1) % ways) for d in range(ways)]
+    down = [(d, (d - 1) % ways) for d in range(ways)]
+    earlier, later = ([x], [x])
+    for _ in range(ways // 2):
+        earlier.append(lax.ppermute(earlier[-1], axis, up))
+    for _ in range((ways - 1) // 2):
+        later.append(lax.ppermute(later[-1], axis, down))
+    line = jnp.concatenate([*earlier[::-1], *later[1:]], axis=dim)
+    return jnp.roll(line, (lax.axis_index(axis) - ways // 2) * x.shape[dim], axis=dim)
 
 
 def split(x):
@@ -38,8 +51,7 @@
     width = total_cols // n_col // CHUNKS
     factor = factor.reshape(-1, CHUNKS, width, block_cols)
     gathered = [
-        lax.all_gather(factor[:, q], "brow", axis=0, tiled=True).reshape(-1, block_cols)
-        for q in range(CHUNKS)
+        gather_around(factor[:, q], "brow", 0).reshape(-1, block_cols) for q in range(CHUNKS)
     ]
     sums = []
     for q in range(CHUNKS):

time: 543 us -> 410 us (0.76)
  waiting for transfers between devices: 411 us -> 239 us
  starting transfers between devices: 0.68 us -> 31.5 us
  other arithmetic: 6.4 us -> 18.3 us
    ppermute x0 -> x12, waiting for transfers between devices: none -> 180 us  [the longest x8 137 us: gather_around(): earlier.append(lax.ppermute(earlier[-1], axis, up))]
    all_gather x4 -> x0, waiting for transfers between devices: 176 us -> none  [local(): lax.all_gather(factor[:, q], 'brow', axis=0, tiled=True)]
    reduce_scatter x4, waiting for transfers between devices: 233 us -> 59.2 us  [local(): sums.append(lax.psum_scatter(part, 'bcol', scatter_dimension=0, tiled=True))]
    ppermute x0 -> x12, starting transfers between devices: none -> 31.3 us  [the longest x8 17.8 us: gather_around(): earlier.append(lax.ppermute(earlier[-1], axis, up))]
    concatenate x0 -> x4, other arithmetic: none -> 11.9 us  [gather_around(): jnp.roll(line, (lax.axis_index(axis) - ways // 2) * x.shape[dim], axis=dim)]
  transfers between devices with their start and end apart: 8 -> 16, of which waited for: 8 -> 13; matrix products, arithmetic and copies ran while one was open for 19% -> 21% of each run, Pallas kernels for 0% -> 0%
where the time goes in v1:
time: 410 us
  waiting for transfers between devices  239 us (58%)
  matrix products  102 us (25%)
  starting transfers between devices  31.5 us (8%)
  other arithmetic  18.3 us (4%)
  between operations  13.3 us (3%)
  local copies, waits for them, and re-layouts  5.49 us (1%)
    ppermute x8, waiting for transfers between devices, gather_around(): earlier.append(lax.ppermute(earlier[-1], axis, up))  137 us
    dot_general x4, matrix products, product(): lax.dot_general(x, y, (((1,), (1,)), ((), ())), preferred_element_type=jn...  102 us
    reduce_scatter x4, waiting for transfers between devices, local(): sums.append(lax.psum_scatter(part, 'bcol', scatter_dimension=0, tiled=True))  59.2 us
    ppermute x4, waiting for transfers between devices, gather_around(): later.append(lax.ppermute(later[-1], axis, down))  43 us
    ppermute x8, starting transfers between devices, gather_around(): earlier.append(lax.ppermute(earlier[-1], axis, up))  17.8 us
    ppermute x4, starting transfers between devices, gather_around(): later.append(lax.ppermute(later[-1], axis, down))  13.5 us
    concatenate x4, other arithmetic, gather_around(): jnp.roll(line, (lax.axis_index(axis) - ways // 2) * x.shape[dim], axis=dim)  11.9 us
  transfers between devices with their start and end apart: 16, of which 13 were waited for; matrix products, arithmetic and copies ran while one was open for 21% of the time, Pallas kernels for 0%

profile of v1, /device:TPU:0, one launch (start us, length us, event | category | flops | bytes accessed | tf_op | source)
XLA Modules:
  0.0 409.5 jit_solution(6713128231130608711)
XLA Ops:
  6.5 0.7 fusion.29
  7.3 0.1 dynamic-slice.7
  7.4 0.5 broadcast_in_dim.19
  7.8 1.3 copy.7
  9.2 2.4 copy.5
  11.6 1.6 bitcast_select_fusion
  13.2 0.3 slice_bitcast_fusion.3
  13.5 3.1 collective-permute-start
  16.6 2.1 collective-permute-start.2
  18.7 18.5 %collective-permute-done = f32[2,48,2048]{2,1,0:T(8,128)} collective-permute-done((f32[2,48,2048]{2,1,0:T(8,128)S(1)}, f32[2,48,2048]{2,1,0:T(8,128)}, u32[]{:S(2)}, u32[]{:S(2)}) %collective-permute-start) | collective-permute-done | bytes 786464 | tf_op jit(solution)/shard_map/ppermute | solution.py:19
  37.2 15.6 %collective-permute-done.2 = f32[2,48,2048]{2,1,0:T(8,128)} collective-permute-done((f32[2,48,2048]{2,1,0:T(8,128)S(1)}, f32[2,48,2048]{2,1,0:T(8,128)}, u32[]{:S(2)}, u32[]{:S(2)}) %collective-permute-start.2) | collective-permute-done | bytes 786464 | tf_op jit(solution)/shard_map/ppermute | solution.py:21
  52.8 17.2 %collective-permute-done.1 = f32[2,48,2048]{2,1,0:T(8,128)} collective-permute-done((f32[2,48,2048]{2,1,0:T(8,128)}, f32[2,48,2048]{2,1,0:T(8,128)}, u32[]{:S(2)}, u32[]{:S(2)}) %collective-permute-start.1) | collective-permute-done | bytes 786464 | tf_op jit(solution)/shard_map/ppermute | solution.py:19
  70.0 3.9 fusion.24
  73.9 25.4 %fusion.30 = f32[384,4096]{1,0:T(8,128)} fusion(f32[384,2048]{1,0:T(8,128)S(1)} %bitcast.29, f32[4096,2048]{1,0:T(8,128)} %param.6), kind=kOutput, calls=%fused_computation.69 | convolution fusion | flops 19327352832 | bytes 42991616 | tf_op jit(solution)/shard_map/dot_general | solution.py:32
  99.3 0.0 reduce-scatter.7.cloned.1.call-start
  99.4 0.1 collective-permute-start.3
  99.4 3.8 collective-permute-start.5
  103.3 18.5 %collective-permute-done.3 = f32[2,48,2048]{2,1,0:T(8,128)S(1)} collective-permute-done((f32[2,48,2048]{2,1,0:T(8,128)S(1)}, f32[2,48,2048]{2,1,0:T(8,128)S(1)}, u32[]{:S(2)}, u32[]{:S(2)}) %collective-permute-start.3) | collective-permute-done | bytes 786464 | tf_op jit(solution)/shard_map/ppermute | solution.py:19
  121.7 15.0 %collective-permute-done.5 = f32[2,48,2048]{2,1,0:T(8,128)S(1)} collective-permute-done((f32[2,48,2048]{2,1,0:T(8,128)S(1)}, f32[2,48,2048]{2,1,0:T(8,128)S(1)}, u32[]{:S(2)}, u32[]{:S(2)}) %collective-permute-start.5) | collective-permute-done | bytes 786464 | tf_op jit(solution)/shard_map/ppermute | solution.py:21
  136.7 15.1 %collective-permute-done.4 = f32[2,48,2048]{2,1,0:T(8,128)S(1)} collective-permute-done((f32[2,48,2048]{2,1,0:T(8,128)S(1)}, f32[2,48,2048]{2,1,0:T(8,128)S(1)}, u32[]{:S(2)}, u32[]{:S(2)}) %collective-permute-start.4) | collective-permute-done | bytes 786464 | tf_op jit(solution)/shard_map/ppermute | solution.py:19
  151.9 2.7 fusion.17
  154.6 25.5 %fusion.31 = f32[384,4096]{1,0:T(8,128)} fusion(f32[384,2048]{1,0:T(8,128)S(1)} %bitcast.30, f32[4096,2048]{1,0:T(8,128)} %param.6), kind=kOutput, calls=%fused_computation.70 | convolution fusion | flops 19327352832 | bytes 42991616 | tf_op jit(solution)/shard_map/dot_general | solution.py:32
  180.1 0.0 reduce-scatter.9.cloned.1.call-start
  180.1 0.1 collective-permute-start.6
  180.2 3.8 collective-permute-start.8
  184.0 18.5 %collective-permute-done.6 = f32[2,48,2048]{2,1,0:T(8,128)S(1)} collective-permute-done((f32[2,48,2048]{2,1,0:T(8,128)S(1)}, f32[2,48,2048]{2,1,0:T(8,128)S(1)}, u32[]{:S(2)}, u32[]{:S(2)}) %collective-permute-start.6) | collective-permute-done | bytes 786464 | tf_op jit(solution)/shard_map/ppermute | solution.py:19
  202.5 6.9 %collective-permute-start.7 = (f32[2,48,2048]{2,1,0:T(8,128)S(1)}, f32[2,48,2048]{2,1,0:T(8,128)S(1)}, u32[]{:S(2)}, u32[]{:S(2)}) collective-permute-start(f32[2,48,2048]{2,1,0:T(8,128)S(1)} %collective-permute-done.6), channel_id=1, source_target_pairs={{0,8},{8,16},{16,24},{24,0},{1,9},{9,17},{17,25},{25,1},{2,10},{10... | collective-permute-start | bytes 2359304 | tf_op jit(solution)/shard_map/ppermute | solution.py:19
  209.4 6.7 %collective-permute-done.8 = f32[2,48,2048]{2,1,0:T(8,128)S(1)} collective-permute-done((f32[2,48,2048]{2,1,0:T(8,128)S(1)}, f32[2,48,2048]{2,1,0:T(8,128)S(1)}, u32[]{:S(2)}, u32[]{:S(2)}) %collective-permute-start.8) | collective-permute-done | bytes 786464 | tf_op jit(solution)/shard_map/ppermute | solution.py:21
  216.1 15.6 %collective-permute-done.7 = f32[2,48,2048]{2,1,0:T(8,128)S(1)} collective-permute-done((f32[2,48,2048]{2,1,0:T(8,128)S(1)}, f32[2,48,2048]{2,1,0:T(8,128)S(1)}, u32[]{:S(2)}, u32[]{:S(2)}) %collective-permute-start.7) | collective-permute-done | bytes 786464 | tf_op jit(solution)/shard_map/ppermute | solution.py:19
  231.7 2.7 fusion.10
  234.4 25.4 %fusion.32 = f32[384,4096]{1,0:T(8,128)} fusion(f32[384,2048]{1,0:T(8,128)S(1)} %bitcast.31, f32[4096,2048]{1,0:T(8,128)} %param.6), kind=kOutput, calls=%fused_computation.71 | convolution fusion | flops 19327352832 | bytes 42991616 | tf_op jit(solution)/shard_map/dot_general | solution.py:32
  259.9 0.0 reduce-scatter.11.cloned.1.call-start
  260.0 0.1 collective-permute-start.9
  260.0 3.8 collective-permute-start.11
  263.8 18.5 %collective-permute-done.9 = f32[2,48,2048]{2,1,0:T(8,128)S(1)} collective-permute-done((f32[2,48,2048]{2,1,0:T(8,128)S(1)}, f32[2,48,2048]{2,1,0:T(8,128)S(1)}, u32[]{:S(2)}, u32[]{:S(2)}) %collective-permute-start.9) | collective-permute-done | bytes 786464 | tf_op jit(solution)/shard_map/ppermute | solution.py:19
  282.3 7.6 %collective-permute-start.10 = (f32[2,48,2048]{2,1,0:T(8,128)S(1)}, f32[2,48,2048]{2,1,0:T(8,128)S(1)}, u32[]{:S(2)}, u32[]{:S(2)}) collective-permute-start(f32[2,48,2048]{2,1,0:T(8,128)S(1)} %collective-permute-done.9), channel_id=1, source_target_pairs={{0,8},{8,16},{16,24},{24,0},{1,9},{9,17},{17,25},{25,1},{2,10},{10... | collective-permute-start | bytes 2359304 | tf_op jit(solution)/shard_map/ppermute | solution.py:19
  289.9 5.7 %collective-permute-done.11 = f32[2,48,2048]{2,1,0:T(8,128)S(1)} collective-permute-done((f32[2,48,2048]{2,1,0:T(8,128)S(1)}, f32[2,48,2048]{2,1,0:T(8,128)S(1)}, u32[]{:S(2)}, u32[]{:S(2)}) %collective-permute-start.11) | collective-permute-done | bytes 786464 | tf_op jit(solution)/shard_map/ppermute | solution.py:21
  295.6 15.0 %collective-permute-done.10 = f32[2,48,2048]{2,1,0:T(8,128)S(1)} collective-permute-done((f32[2,48,2048]{2,1,0:T(8,128)S(1)}, f32[2,48,2048]{2,1,0:T(8,128)S(1)}, u32[]{:S(2)}, u32[]{:S(2)}) %collective-permute-start.10) | collective-permute-done | bytes 786464 | tf_op jit(solution)/shard_map/ppermute | solution.py:19
  310.6 2.7 fusion.3
  313.3 25.5 %fusion.33 = f32[384,4096]{1,0:T(8,128)} fusion(f32[384,2048]{1,0:T(8,128)S(1)} %bitcast.28, f32[4096,2048]{1,0:T(8,128)} %param.6), kind=kOutput, calls=%fused_computation.72 | convolution fusion | flops 19327352832 | bytes 42991616 | tf_op jit(solution)/shard_map/dot_general | solution.py:32
  338.8 0.1 dynamic-slice.6
  338.9 0.3 broadcast_in_dim.18
  339.2 0.5 copy.6
  339.7 0.0 reduce-scatter.5.cloned.1.call-done
  339.7 0.0 reduce-scatter.7.cloned.1.call-done
  339.8 0.0 reduce-scatter.9.cloned.1.call-done
  339.8 59.2 %reduce-scatter.11.cloned.1.call-done = f32[48,4096]{1,0:T(8,128)} async-done(((f32[384,4096]{1,0:T(8,128)}), f32[48,4096]{1,0:T(8,128)}) %reduce-scatter.11.cloned.1.call-update) | async-done | bytes 786448 | tf_op jit(solution)/shard_map/reduce_scatter | solution.py:59
  399.0 4.0 fusion.28
  (7 shorter events, 0.1 us)
Async XLA Ops:
  6.5 333.2 %reduce-scatter.5.cloned.1.call-start = ((), (), s32[]{:S(2)}) async-start(), calls=%async_computation.4 | async-start | bytes 7077888 | tf_op jit(solution)/shard_map/reduce_scatter | solution.py:59
  13.5 23.6 %collective-permute-start = (f32[2,48,2048]{2,1,0:T(8,128)S(1)}, f32[2,48,2048]{2,1,0:T(8,128)}, u32[]{:S(2)}, u32[]{:S(2)}) collective-permute-start(f32[2,48,2048]{2,1,0:T(8,128)S(1)} %get-tuple-element.6), channel_id=1, source_target_pairs={{0,8},{8,16},{16,24},{24,0},{1,9},{9,17},{17,25},{25,1},{2,10},{10... | collective-permute-start | bytes 2359304 | tf_op jit(solution)/shard_map/ppermute | solution.py:19
  16.6 36.2 %collective-permute-start.2 = (f32[2,48,2048]{2,1,0:T(8,128)S(1)}, f32[2,48,2048]{2,1,0:T(8,128)}, u32[]{:S(2)}, u32[]{:S(2)}) collective-permute-start(f32[2,48,2048]{2,1,0:T(8,128)S(1)} %get-tuple-element.6), channel_id=1, source_target_pairs={{0,24},{8,0},{16,8},{24,16},{1,25},{9,1},{17,9},{25,17},{2,26},{10... | collective-permute-start | bytes 2359304 | tf_op jit(solution)/shard_map/ppermute | solution.py:21
  37.2 32.9 %collective-permute-start.1 = (f32[2,48,2048]{2,1,0:T(8,128)}, f32[2,48,2048]{2,1,0:T(8,128)}, u32[]{:S(2)}, u32[]{:S(2)}) collective-permute-start(f32[2,48,2048]{2,1,0:T(8,128)} %collective-permute-done), channel_id=1, source_target_pairs={{0,8},{8,16},{16,24},{24,0},{1,9},{9,17},{17,25},{25,1},{2,10},{10... | collective-permute-start | bytes 2359304 | tf_op jit(solution)/shard_map/ppermute | solution.py:19
  99.3 240.4 %reduce-scatter.7.cloned.1.call-start = ((), (), s32[]{:S(2)}) async-start(), calls=%async_computation.5 | async-start | bytes 7077888 | tf_op jit(solution)/shard_map/reduce_scatter | solution.py:59
  99.4 22.3 %collective-permute-start.3 = (f32[2,48,2048]{2,1,0:T(8,128)S(1)}, f32[2,48,2048]{2,1,0:T(8,128)S(1)}, u32[]{:S(2)}, u32[]{:S(2)}) collective-permute-start(f32[2,48,2048]{2,1,0:T(8,128)S(1)} %get-tuple-element.9), channel_id=1, source_target_pairs={{0,8},{8,16},{16,24},{24,0},{1,9},{9,17},{17,25},{25,1},{2,10},{10... | collective-permute-start | bytes 2359304 | tf_op jit(solution)/shard_map/ppermute | solution.py:19
  99.4 37.3 %collective-permute-start.5 = (f32[2,48,2048]{2,1,0:T(8,128)S(1)}, f32[2,48,2048]{2,1,0:T(8,128)S(1)}, u32[]{:S(2)}, u32[]{:S(2)}) collective-permute-start(f32[2,48,2048]{2,1,0:T(8,128)S(1)} %get-tuple-element.9), channel_id=1, source_target_pairs={{0,24},{8,0},{16,8},{24,16},{1,25},{9,1},{17,9},{25,17},{2,26},{10... | collective-permute-start | bytes 2359304 | tf_op jit(solution)/shard_map/ppermute | solution.py:21
  121.7 30.2 %collective-permute-start.4 = (f32[2,48,2048]{2,1,0:T(8,128)S(1)}, f32[2,48,2048]{2,1,0:T(8,128)S(1)}, u32[]{:S(2)}, u32[]{:S(2)}) collective-permute-start(f32[2,48,2048]{2,1,0:T(8,128)S(1)} %collective-permute-done.3), channel_id=1, source_target_pairs={{0,8},{8,16},{16,24},{24,0},{1,9},{9,17},{17,25},{25,1},{2,10},{10... | collective-permute-start | bytes 2359304 | tf_op jit(solution)/shard_map/ppermute | solution.py:19
  180.1 159.7 %reduce-scatter.9.cloned.1.call-start = ((), (), s32[]{:S(2)}) async-start(), calls=%async_computation.6 | async-start | bytes 7077888 | tf_op jit(solution)/shard_map/reduce_scatter | solution.py:59
  180.1 22.3 %collective-permute-start.6 = (f32[2,48,2048]{2,1,0:T(8,128)S(1)}, f32[2,48,2048]{2,1,0:T(8,128)S(1)}, u32[]{:S(2)}, u32[]{:S(2)}) collective-permute-start(f32[2,48,2048]{2,1,0:T(8,128)S(1)} %get-tuple-element.8), channel_id=1, source_target_pairs={{0,8},{8,16},{16,24},{24,0},{1,9},{9,17},{17,25},{25,1},{2,10},{10... | collective-permute-start | bytes 2359304 | tf_op jit(solution)/shard_map/ppermute | solution.py:19
  180.2 35.9 %collective-permute-start.8 = (f32[2,48,2048]{2,1,0:T(8,128)S(1)}, f32[2,48,2048]{2,1,0:T(8,128)S(1)}, u32[]{:S(2)}, u32[]{:S(2)}) collective-permute-start(f32[2,48,2048]{2,1,0:T(8,128)S(1)} %get-tuple-element.8), channel_id=1, source_target_pairs={{0,24},{8,0},{16,8},{24,16},{1,25},{9,1},{17,9},{25,17},{2,26},{10... | collective-permute-start | bytes 2359304 | tf_op jit(solution)/shard_map/ppermute | solution.py:21
  202.5 29.3 %collective-permute-start.7 = (f32[2,48,2048]{2,1,0:T(8,128)S(1)}, f32[2,48,2048]{2,1,0:T(8,128)S(1)}, u32[]{:S(2)}, u32[]{:S(2)}) collective-permute-start(f32[2,48,2048]{2,1,0:T(8,128)S(1)} %collective-permute-done.6), channel_id=1, source_target_pairs={{0,8},{8,16},{16,24},{24,0},{1,9},{9,17},{17,25},{25,1},{2,10},{10... | collective-permute-start | bytes 2359304 | tf_op jit(solution)/shard_map/ppermute | solution.py:19
  259.9 139.1 %reduce-scatter.11.cloned.1.call-start = ((), (), s32[]{:S(2)}) async-start(), calls=%async_computation.7 | async-start | bytes 7077888 | tf_op jit(solution)/shard_map/reduce_scatter | solution.py:59
  260.0 22.3 %collective-permute-start.9 = (f32[2,48,2048]{2,1,0:T(8,128)S(1)}, f32[2,48,2048]{2,1,0:T(8,128)S(1)}, u32[]{:S(2)}, u32[]{:S(2)}) collective-permute-start(f32[2,48,2048]{2,1,0:T(8,128)S(1)} %get-tuple-element.7), channel_id=1, source_target_pairs={{0,8},{8,16},{16,24},{24,0},{1,9},{9,17},{17,25},{25,1},{2,10},{10... | collective-permute-start | bytes 2359304 | tf_op jit(solution)/shard_map/ppermute | solution.py:19
  260.0 35.6 %collective-permute-start.11 = (f32[2,48,2048]{2,1,0:T(8,128)S(1)}, f32[2,48,2048]{2,1,0:T(8,128)S(1)}, u32[]{:S(2)}, u32[]{:S(2)}) collective-permute-start(f32[2,48,2048]{2,1,0:T(8,128)S(1)} %get-tuple-element.7), channel_id=1, source_target_pairs={{0,24},{8,0},{16,8},{24,16},{1,25},{9,1},{17,9},{25,17},{2,26},{10... | collective-permute-start | bytes 2359304 | tf_op jit(solution)/shard_map/ppermute | solution.py:21
  282.3 28.3 %collective-permute-start.10 = (f32[2,48,2048]{2,1,0:T(8,128)S(1)}, f32[2,48,2048]{2,1,0:T(8,128)S(1)}, u32[]{:S(2)}, u32[]{:S(2)}) collective-permute-start(f32[2,48,2048]{2,1,0:T(8,128)S(1)} %collective-permute-done.9), channel_id=1, source_target_pairs={{0,8},{8,16},{16,24},{24,0},{1,9},{9,17},{17,25},{25,1},{2,10},{10... | collective-permute-start | bytes 2359304 | tf_op jit(solution)/shard_map/ppermute | solution.py:19
Sparse Core Ops, SparseCore 0:
  99.4 61.0 reduce-scatter.4
  180.2 59.9 reduce-scatter.6
  260.0 59.9 reduce-scatter.8
  338.9 59.9 reduce-scatter.10
